TPU v7x, 32 devices: a whole 2x2x4 slice. The times are simulated.
32 devices in a mesh: chan: 16 (over z, x, core), rows: 2 (over y).
Axes of the slice: x: 2, y: 2, z: 4, core: 2. Of those that a mesh axis runs over, the one named last changes fastest.
Arguments:
- image: bfloat16 [768, 1, 32, 128], P('chan', None, 'rows'), may hold values from -3 to 3
- dw_kernel: float32 [768, 7, 7], P('chan'), may hold values from -13 to 13
- ln_gain: float32 [768], P('chan'), may hold values from 0.1 to 1.9
- w_in: bfloat16 [768, 3072], P(None, 'chan'), may hold values from -0.21875 to 0.21875
- w_out: bfloat16 [3072, 768], P('chan'), may hold values from -0.15625 to 0.15625
- layer_scale: float32 [768], P('chan'), may hold values from 0.3 to 1
- cotangent: bfloat16 [768, 1, 32, 128], P('chan', None, 'rows'), may hold values from -6 to 6
Outputs:
- block_out: bfloat16 [768, 1, 32, 128], P('chan', None, 'rows')
- grad_image: bfloat16 [768, 1, 32, 128], P('chan', None, 'rows')
- grad_kernel: float32 [768, 7, 7], P('chan')
- grad_gain: float32 [768], P('chan')
- grad_scale: float32 [768], P('chan')
- grad_w_in: float32 [768, 3072], P(None, 'chan')
- grad_w_out: float32 [3072, 768], P('chan')
All inputs are finite; a program needn't handle non-finite values.
Results may differ from a plain program's by a relative error of at most 0.018.
Values may be sent and summed in bfloat16 or wider, within the bound.
A program may use at most 64 MiB of HBM per device.

v0:
```python
import jax
import jax.numpy as jnp
from jax import lax
from jax.sharding import PartitionSpec as P

D = 768
KSIZE = 7
epsilon = 1e-06
inv_root_two = 0.7071067811865476
inv_root_two_pi = 0.3989422804014327


def extended(block, sides, width):
    for axis, dim in sides:
        count = lax.axis_size(axis)
        forward = [(i, i + 1) for i in range(count - 1)]
        backward = [(target, source) for source, target in forward]
        low = lax.ppermute(
            lax.slice_in_dim(block, block.shape[dim] - width, None, axis=dim), axis, forward
        )
        high = lax.ppermute(lax.slice_in_dim(block, 0, width, axis=dim), axis, backward)
        block = jnp.concatenate([low, block, high], axis=dim)
    return block


def gelu_slope(values):
    return (
        0.5 * (1.0 + lax.erf(values * inv_root_two))
        + values * jnp.exp(-0.5 * values * values) * inv_root_two_pi
    )


def forward_taps(padded, kernel, height, breadth):
    running = jnp.zeros((padded.shape[0], padded.shape[1], height, breadth), jnp.float32)
    for u in range(KSIZE):
        for v in range(KSIZE):
            running = (
                running
                + kernel[:, u, v][:, None, None, None]
                * padded[:, :, u : u + height, v : v + breadth]
            )
    return running


def transpose_taps(padded, kernel, height, breadth):
    running = jnp.zeros((padded.shape[0], padded.shape[1], height, breadth), jnp.float32)
    for u in range(KSIZE):
        for v in range(KSIZE):
            running = (
                running
                + kernel[:, u, v][:, None, None, None]
                * padded[:, :, 6 - u : 6 - u + height, 6 - v : 6 - v + breadth]
            )
    return running


def correlate_taps(padded, grad, height, breadth):
    columns = []
    for u in range(KSIZE):
        row_terms = []
        for v in range(KSIZE):
            row_terms.append(
                jnp.sum(grad * padded[:, :, u : u + height, v : v + breadth], axis=(1, 2, 3))
            )
        columns.append(jnp.stack(row_terms, axis=1))
    return jnp.stack(columns, axis=1)


def body(image, dw_kernel, ln_gain, w_in, w_out, layer_scale, cotangent):
    channels, images, height, breadth = image.shape
    pixels = images * height * breadth
    contract_lead = (((0,), (0,)), ((), ()))
    contract_tail = (((1,), (1,)), ((), ()))
    rimmed_image = extended(image, (("rows", 2),), 3)
    padded = jnp.pad(rimmed_image.astype(jnp.float32), ((0, 0), (0, 0), (0, 0), (3, 3)))
    mixed_in = forward_taps(padded, dw_kernel, height, breadth).astype(jnp.bfloat16)
    mixed_flat = mixed_in.reshape(channels, pixels).astype(jnp.float32)
    centre = lax.psum(jnp.sum(mixed_flat, axis=0), "chan") / D
    spread = lax.psum(jnp.sum(jnp.square(mixed_flat - centre), axis=0), "chan") / D
    inv_scale = lax.rsqrt(spread + epsilon)
    unit_norm = (mixed_flat - centre) * inv_scale
    normed = (unit_norm * ln_gain[:, None]).astype(jnp.bfloat16)
    weight_cut = w_in
    pre_act = lax.dot_general(
        weight_cut,
        lax.all_gather(normed, "chan", axis=0, tiled=True),
        contract_lead,
        preferred_element_type=jnp.float32,
    )
    activated = jax.nn.gelu(pre_act, approximate=False).astype(jnp.bfloat16)
    weight_cut = w_out
    branch = lax.psum_scatter(
        lax.dot_general(
            weight_cut, activated, contract_lead, preferred_element_type=jnp.float32
        ).astype(jnp.bfloat16),
        "chan",
        scatter_dimension=0,
        tiled=True,
    ).astype(jnp.float32)
    image_flat = image.reshape(channels, pixels).astype(jnp.float32)
    block_out = (
        (image_flat + layer_scale[:, None] * branch).astype(jnp.bfloat16).reshape(image.shape)
    )
    cotan_flat = cotangent.reshape(channels, pixels).astype(jnp.float32)
    scaled = (layer_scale[:, None] * cotan_flat).astype(jnp.bfloat16)
    portion = lax.all_gather(scaled, "chan", axis=0, tiled=True)
    weight_cut = w_out
    grad_run = jnp.dot(weight_cut, portion, preferred_element_type=jnp.float32)
    column_block = lax.dot_general(
        activated, portion, contract_tail, preferred_element_type=jnp.float32
    )
    grad_w_out = column_block
    grad_scale = jnp.sum(cotan_flat * branch, axis=1)
    grad_pre = (grad_run * gelu_slope(pre_act)).astype(jnp.bfloat16)
    grad_w_in = lax.dot_general(
        lax.all_gather(normed, "chan", axis=0, tiled=True),
        grad_pre,
        contract_tail,
        preferred_element_type=jnp.float32,
    )
    weight_cut = w_in
    grad_normed = lax.psum_scatter(
        jnp.dot(weight_cut, grad_pre, preferred_element_type=jnp.float32).astype(jnp.bfloat16),
        "chan",
        scatter_dimension=0,
        tiled=True,
    ).astype(jnp.float32)
    grad_gain = jnp.sum(grad_normed * unit_norm, axis=1)
    scaled_grad = grad_normed * ln_gain[:, None]
    total_one, total_two = lax.psum(
        (jnp.sum(scaled_grad, axis=0), jnp.sum(scaled_grad * unit_norm, axis=0)), "chan"
    )
    grad_mixed = (inv_scale * (scaled_grad - total_one / D - unit_norm * (total_two / D))).astype(
        jnp.bfloat16
    )
    grad_mixed = grad_mixed.reshape(channels, images, height, breadth)
    rimmed_grad = extended(grad_mixed, (("rows", 2),), 3)
    rimmed_grad = jnp.pad(rimmed_grad.astype(jnp.float32), ((0, 0), (0, 0), (0, 0), (3, 3)))
    spread_back = transpose_taps(rimmed_grad, dw_kernel, height, breadth)
    grad_image = (cotangent.astype(jnp.float32) + spread_back).astype(jnp.bfloat16)
    grad_kernel = correlate_taps(padded, grad_mixed.astype(jnp.float32), height, breadth)
    grad_w_in, grad_w_out, grad_kernel, grad_gain, grad_scale = (
        lax.psum(grad_w_in.astype(jnp.bfloat16), "rows").astype(jnp.float32),
        lax.psum(grad_w_out.astype(jnp.bfloat16), "rows").astype(jnp.float32),
        lax.psum(grad_kernel.astype(jnp.bfloat16), "rows").astype(jnp.float32),
        lax.psum(grad_gain.astype(jnp.bfloat16), "rows").astype(jnp.float32),
        lax.psum(grad_scale.astype(jnp.bfloat16), "rows").astype(jnp.float32),
    )
    return (block_out, grad_image, grad_kernel, grad_gain, grad_scale, grad_w_in, grad_w_out)


def solution(mesh):
    return jax.shard_map(
        body,
        mesh=mesh,
        in_specs=(
            P("chan", None, "rows", None),
            P("chan", None, None),
            P("chan"),
            P(None, "chan"),
            P("chan", None),
            P("chan"),
            P("chan", None, "rows", None),
        ),
        out_specs=(
            P("chan", None, "rows", None),
            P("chan", None, "rows", None),
            P("chan", None, None),
            P("chan"),
            P("chan"),
            P(None, "chan"),
            P("chan", None),
        ),
        check_vma=False,
    )
```

profile of v0, /device:TPU:0, one launch (start us, length us, event | category | flops | bytes accessed | tf_op | source)
XLA Modules:
  0.0 478.2 jit_solution(16257528177359169895)
XLA Ops:
  8.2 4.9 %collective-permute-start = (bf16[48,1,3,128]{3,2,1,0:T(4,128)(2,1)S(1)}, bf16[48,1,3,128]{3,2,1,0:T(4,128)(2,1)S(1)}, u32[]{:S(2)}, u32[]{:S(2)}) collective-permute-start(bf16[48,1,3,128]{3,2,1,0:T(4,128)(2,1)S(1)} %get-tuple-element.87), channel_id=1, source_target_pairs={{0,1},{2,3},{4,5},{6,7},{8,9},{10,11},{12,13},{14,15},{16,17},{18,... | collective-permute-start | bytes 110600 | tf_op jit(solution)/shard_map/ppermute | solution.py:18
  13.1 1.3 collective-permute-start.1
  16.7 1.5 slice_bitcast_fusion.46
  20.2 8.4 %convert_reduce_fusion = (f32[16,128]{1,0:T(8,128)S(1)}, bf16[48,1,16,128]{3,2,1,0:T(8,128)(2,1)S(1)}) fusion(f32[48]{0:T(128)} %get-tuple-element.136, f32[48]{0:T(128)} %get-tuple-element.137, f32[48]{0:T(128)S(1)} %get-tuple-element.90, f32[48,1,22,128]{3,2,1,0:T(8,128)S(1)} %maximum_convert_fusion, f32[48]{0:T(128)S(1)} %get-tuple-element.91, ...), kind=kLoop, calls=%fused_computation.340 | loop fusion | flops 9828352 | bytes 3571264 | tf_op jit(solution)/shard_map/reduce_sum | solution.py:78
  29.0 32.9 %psum.63 = f32[2048]{0:T(1024)S(1)} all-reduce(f32[2048]{0:T(1024)S(1)} %bitcast.426), channel_id=1, replica_groups=mesh['chan'=16,'rows'=2] {'chan'}, use_global_device_ids=true, to_apply=%region_1.2 | all-reduce | flops 2048 | bytes 16384 | tf_op jit(solution)/shard_map/psum | solution.py:78
  61.9 30.0 %psum.64 = f32[2048]{0:T(1024)S(1)} all-reduce(f32[2048]{0:T(1024)S(1)} %bitcast.427), channel_id=1, replica_groups=mesh['chan'=16,'rows'=2] {'chan'}, use_global_device_ids=true, to_apply=%region_3.4 | all-reduce | flops 2048 | bytes 16384 | tf_op jit(solution)/shard_map/psum | solution.py:79
  92.9 43.4 %all-gather.3.cloned.1.call-done = bf16[768,2048]{1,0:T(8,128)(2,1)} async-done(((bf16[48,2048]{1,0:T(8,128)(2,1)}), bf16[768,2048]{1,0:T(8,128)(2,1)}) %all-gather.3.cloned.1.call-update) | async-done | bytes 3145744 | tf_op jit(solution)/shard_map/all_gather | solution.py:86
  136.3 6.8 %fusion.6 = (bf16[192,2048]{1,0:T(8,128)(2,1)S(1)}, f32[192,2048]{1,0:T(8,128)}) fusion(bf16[768,192]{0,1:T(8,128)(2,1)S(1)} %copy-done, bf16[768,2048]{1,0:T(8,128)(2,1)} %all-gather.3.cloned.1.call-done), kind=kOutput, calls=%fused_computation.145 | convolution fusion | flops 629538816 | bytes 5799936 | tf_op jit(solution)/shard_map/dot_general | solution.py:84
  143.1 2.7 fusion
  145.8 4.7 copy.31
  153.0 62.7 %reduce-scatter.7.cloned.1.call-done = bf16[48,2048]{1,0:T(8,128)(2,1)} async-done(((bf16[768,2048]{1,0:T(8,128)(2,1)}), bf16[48,2048]{1,0:T(8,128)(2,1)}) %reduce-scatter.7.cloned.1.call-update) | async-done | bytes 196624
  215.7 1.9 copy.32
  217.7 2.6 fusion.20
  220.3 1.9 copy.24
  222.5 44.0 %all-gather.5.cloned.1.call-done = bf16[768,2048]{1,0:T(8,128)(2,1)} async-done(((bf16[48,2048]{1,0:T(8,128)(2,1)}), bf16[768,2048]{1,0:T(8,128)(2,1)}) %all-gather.5.cloned.1.call-update) | async-done | bytes 3145744 | tf_op jit(solution)/shard_map/all_gather | solution.py:106
  266.5 4.0 convolution_convert_fusion.2
  270.4 2.8 fusion.3
  273.2 2.0 convolution_convert_fusion.3
  275.3 2.7 fusion.1
  278.0 4.8 copy.33
  284.7 19.7 %all-reduce.7.cloned.1.call-done = (bf16[768,192]{0,1:T(8,128)(2,1)}, bf16[192,768]{1,0:T(8,128)(2,1)}) async-done(((bf16[768,192]{0,1:T(8,128)(2,1)}, bf16[192,768]{1,0:T(8,128)(2,1)}), (bf16[768,192]{0,1:T(8,128)(2,1)}, bf16[192,768]{1,0:T(8,128)(2,1)})) %all-reduce.7.cloned.1.call-update) | async-done | bytes 589840 | tf_op jit(solution)/shard_map/psum | solution.py:143
  304.4 1.8 convert_element_type.162
  306.2 1.8 convert_element_type.164
  308.0 66.8 %reduce-scatter.9.cloned.1.call-done = bf16[48,2048]{1,0:T(8,128)(2,1)} async-done(((bf16[768,2048]{1,0:T(8,128)(2,1)}), bf16[48,2048]{1,0:T(8,128)(2,1)}) %reduce-scatter.9.cloned.1.call-update) | async-done | bytes 196624 | tf_op jit(solution)/shard_map/reduce_scatter | solution.py:122
  376.1 57.7 %all-reduce.2 = (f32[2048]{0:T(1024)S(1)}, f32[2048]{0:T(1024)S(1)}) all-reduce(f32[2048]{0:T(1024)S(1)} %get-tuple-element.71, f32[2048]{0:T(1024)S(1)} %get-tuple-element.72), channel_id=1, replica_groups=mesh['chan'=16,'rows'=2] {'chan'}, use_global_device_ids=true, to_apply=%region_9.10 | all-reduce | flops 4096 | bytes 32768 | tf_op jit(solution)/shard_map/psum | solution.py:130
  434.9 4.3 fusion.78
  439.2 4.2 fusion.77
  443.8 2.3 fusion.76
  446.2 3.4 collective-permute-start.2
  449.6 1.3 collective-permute-start.3
  451.1 9.2 %all-reduce.3 = (bf16[48,7,7]{0,2,1:T(8,128)(2,1)S(1)}, bf16[48]{0:T(256)(128)(2,1)S(1)}, bf16[48]{0:T(256)(128)(2,1)S(1)}) all-reduce(bf16[48,7,7]{0,2,1:T(8,128)(2,1)S(1)} %constant_dynamic-update-slice_fusion, bf16[48]{0:T(256)(128)(2,1)S(1)} %get-tuple-element.70, ...), channel_id=1, replica_groups=mesh['chan'=16,'rows'=2] {'rows'}, use_global_device_ids=true, to_apply=%region_59.60 | all-reduce | flops 2448 | bytes 9792 | tf_op jit(solution)/shard_map/psum | solution.py:145
  462.6 9.1 %fusion.166 = bf16[48,1,16,128]{3,2,1,0:T(8,128)(2,1)} fusion(f32[48,1,22,128]{3,2,1,0:T(8,128)S(1)} %maximum_convert_fusion.1, f32[48]{0:T(128)} %get-tuple-element.136, f32[48]{0:T(128)} %get-tuple-element.137, f32[48]{0:T(128)S(1)} %get-tuple-element.90, f32[48]{0:T(128)S(1)} %get-tuple-element.91, f32[48]{0:T(128)S(1)} %get-tuple-element.92, ...), kind=kLoop, calls=%fused_computation.320 | loop fusion | flops 9830400 | bytes 3759680 | tf_op jit(solution)/shard_map/convert_element_type | solution.py:140
  (223 shorter events, 15.5 us)
Async XLA Ops:
  7.2 129.1 %copy-start = (bf16[768,192]{0,1:T(8,128)(2,1)S(1)}, bf16[768,192]{0,1:T(8,128)(2,1)}, u32[]{:S(2)}) copy-start(bf16[768,192]{0,1:T(8,128)(2,1)} %param.10) | copy-start | bytes 884740
  7.2 129.1 %all-gather.3.cloned.1.call-start = ((), (), s32[]{:S(2)}) async-start(), calls=%async_computation.2 | async-start | bytes 3342336 | tf_op jit(solution)/shard_map/all_gather | solution.py:86
  8.2 10.0 %collective-permute-start = (bf16[48,1,3,128]{3,2,1,0:T(4,128)(2,1)S(1)}, bf16[48,1,3,128]{3,2,1,0:T(4,128)(2,1)S(1)}, u32[]{:S(2)}, u32[]{:S(2)}) collective-permute-start(bf16[48,1,3,128]{3,2,1,0:T(4,128)(2,1)S(1)} %get-tuple-element.87), channel_id=1, source_target_pairs={{0,1},{2,3},{4,5},{6,7},{8,9},{10,11},{12,13},{14,15},{16,17},{18,... | collective-permute-start | bytes 110600 | tf_op jit(solution)/shard_map/ppermute | solution.py:18
  13.1 6.0 %collective-permute-start.1 = (bf16[48,1,3,128]{3,2,1,0:T(4,128)(2,1)S(1)}, bf16[48,1,3,128]{3,2,1,0:T(4,128)(2,1)S(1)}, u32[]{:S(2)}, u32[]{:S(2)}) collective-permute-start(bf16[48,1,3,128]{3,2,1,0:T(4,128)(2,1)S(1)} %get-tuple-element.88), channel_id=1, source_target_pairs={{1,0},{3,2},{5,4},{7,6},{9,8},{11,10},{13,12},{15,14},{17,16},{19,... | collective-permute-start | bytes 110600 | tf_op jit(solution)/shard_map/ppermute | solution.py:21
  20.2 71.8 %copy-start.7 = (f32[48]{0:T(128)S(1)}, f32[48]{0:T(128)}, u32[]{:S(2)}) copy-start(f32[48]{0:T(128)} %param.9) | copy-start | bytes 580
  92.8 50.3 %copy-start.5 = (bf16[192,768]{1,0:T(8,128)(2,1)S(1)}, bf16[192,768]{1,0:T(8,128)(2,1)}, u32[]{:S(2)}) copy-start(bf16[192,768]{1,0:T(8,128)(2,1)} %param.11) | copy-start | bytes 884740
  92.8 122.9 %reduce-scatter.7.cloned.1.call-start = ((), (), s32[]{:S(2)}) async-start(), calls=%async_computation.4 | async-start | bytes 3342336
  150.5 115.9 %all-gather.5.cloned.1.call-start = ((), (), s32[]{:S(2)}) async-start(), calls=%async_computation.3 | async-start | bytes 3342336 | tf_op jit(solution)/shard_map/all_gather | solution.py:106
  222.2 48.2 %copy-start.6 = (bf16[192,768]{1,0:T(8,128)(2,1)S(1)}, bf16[192,768]{1,0:T(8,128)(2,1)}, u32[]{:S(2)}) copy-start(bf16[192,768]{1,0:T(8,128)(2,1)} %param.11) | copy-start | bytes 884740
  222.2 82.2 %all-reduce.7.cloned.1.call-start = ((), (), s32[]{:S(2)}) async-start(), calls=%async_computation.6 | async-start | bytes 1179648 | tf_op jit(solution)/shard_map/psum | solution.py:143
  275.2 99.6 %reduce-scatter.9.cloned.1.call-start = ((), (), s32[]{:S(2)}) async-start(), calls=%async_computation.5 | async-start | bytes 3342336 | tf_op jit(solution)/shard_map/reduce_scatter | solution.py:122
  443.4 18.8 %copy-start.9 = (f32[48]{0:T(128)S(1)}, f32[48]{0:T(128)}, u32[]{:S(2)}) copy-start(f32[48]{0:T(128)} %copy-done.8) | copy-start | bytes 580
  443.4 18.8 %copy-start.11 = (f32[48]{0:T(128)S(1)}, f32[48]{0:T(128)}, u32[]{:S(2)}) copy-start(f32[48]{0:T(128)} %copy-done.10) | copy-start | bytes 580
  443.4 18.8 %copy-start.13 = (f32[48]{0:T(128)S(1)}, f32[48]{0:T(128)}, u32[]{:S(2)}) copy-start(f32[48]{0:T(128)} %copy-done.12) | copy-start | bytes 580
  443.4 18.8 %copy-start.15 = (f32[48]{0:T(128)S(1)}, f32[48]{0:T(128)}, u32[]{:S(2)}) copy-start(f32[48]{0:T(128)} %copy-done.14) | copy-start | bytes 580
  443.5 18.8 %copy-start.17 = (f32[48]{0:T(128)S(1)}, f32[48]{0:T(128)}, u32[]{:S(2)}) copy-start(f32[48]{0:T(128)} %copy-done.16) | copy-start | bytes 580
  443.5 18.8 %copy-start.19 = (f32[48]{0:T(128)S(1)}, f32[48]{0:T(128)}, u32[]{:S(2)}) copy-start(f32[48]{0:T(128)} %copy-done.18) | copy-start | bytes 580
  443.5 18.8 %copy-start.21 = (f32[48]{0:T(128)S(1)}, f32[48]{0:T(128)}, u32[]{:S(2)}) copy-start(f32[48]{0:T(128)} %copy-done.20) | copy-start | bytes 580
  443.5 18.8 %copy-start.23 = (f32[48]{0:T(128)S(1)}, f32[48]{0:T(128)}, u32[]{:S(2)}) copy-start(f32[48]{0:T(128)} %copy-done.22) | copy-start | bytes 580
  443.5 18.8 %copy-start.25 = (f32[48]{0:T(128)S(1)}, f32[48]{0:T(128)}, u32[]{:S(2)}) copy-start(f32[48]{0:T(128)} %copy-done.24) | copy-start | bytes 580
  443.5 18.8 %copy-start.27 = (f32[48]{0:T(128)S(1)}, f32[48]{0:T(128)}, u32[]{:S(2)}) copy-start(f32[48]{0:T(128)} %copy-done.26) | copy-start | bytes 580
  443.5 18.8 %copy-start.29 = (f32[48]{0:T(128)S(1)}, f32[48]{0:T(128)}, u32[]{:S(2)}) copy-start(f32[48]{0:T(128)} %copy-done.28) | copy-start | bytes 580
  443.5 18.8 %copy-start.31 = (f32[48]{0:T(128)S(1)}, f32[48]{0:T(128)}, u32[]{:S(2)}) copy-start(f32[48]{0:T(128)} %copy-done.30) | copy-start | bytes 580
  443.5 18.8 %copy-start.33 = (f32[48]{0:T(128)S(1)}, f32[48]{0:T(128)}, u32[]{:S(2)}) copy-start(f32[48]{0:T(128)} %copy-done.32) | copy-start | bytes 580
  443.5 18.8 %copy-start.35 = (f32[48]{0:T(128)S(1)}, f32[48]{0:T(128)}, u32[]{:S(2)}) copy-start(f32[48]{0:T(128)} %copy-done.34) | copy-start | bytes 580
  443.6 18.8 %copy-start.37 = (f32[48]{0:T(128)S(1)}, f32[48]{0:T(128)}, u32[]{:S(2)}) copy-start(f32[48]{0:T(128)} %copy-done.36) | copy-start | bytes 580
  443.6 18.8 %copy-start.39 = (f32[48]{0:T(128)S(1)}, f32[48]{0:T(128)}, u32[]{:S(2)}) copy-start(f32[48]{0:T(128)} %copy-done.38) | copy-start | bytes 580
  443.6 18.8 %copy-start.41 = (f32[48]{0:T(128)S(1)}, f32[48]{0:T(128)}, u32[]{:S(2)}) copy-start(f32[48]{0:T(128)} %copy-done.40) | copy-start | bytes 580
  443.6 18.8 %copy-start.43 = (f32[48]{0:T(128)S(1)}, f32[48]{0:T(128)}, u32[]{:S(2)}) copy-start(f32[48]{0:T(128)} %copy-done.42) | copy-start | bytes 580
  443.6 18.8 %copy-start.45 = (f32[48]{0:T(128)S(1)}, f32[48]{0:T(128)}, u32[]{:S(2)}) copy-start(f32[48]{0:T(128)} %copy-done.44) | copy-start | bytes 580
  446.2 15.8 %collective-permute-start.2 = (bf16[48,1,3,128]{3,2,1,0:T(4,128)(2,1)S(1)}, bf16[48,1,3,128]{3,2,1,0:T(4,128)(2,1)S(1)}, u32[]{:S(2)}, u32[]{:S(2)}) collective-permute-start(bf16[48,1,3,128]{3,2,1,0:T(4,128)(2,1)S(1)} %get-tuple-element.85), channel_id=1, source_target_pairs={{0,1},{2,3},{4,5},{6,7},{8,9},{10,11},{12,13},{14,15},{16,17},{18,... | collective-permute-start | bytes 110600 | tf_op jit(solution)/shard_map/ppermute | solution.py:18
  449.6 12.4 %collective-permute-start.3 = (bf16[48,1,3,128]{3,2,1,0:T(4,128)(2,1)S(1)}, bf16[48,1,3,128]{3,2,1,0:T(4,128)(2,1)S(1)}, u32[]{:S(2)}, u32[]{:S(2)}) collective-permute-start(bf16[48,1,3,128]{3,2,1,0:T(4,128)(2,1)S(1)} %get-tuple-element.86), channel_id=1, source_target_pairs={{1,0},{3,2},{5,4},{7,6},{9,8},{11,10},{13,12},{15,14},{17,16},{19,... | collective-permute-start | bytes 110600 | tf_op jit(solution)/shard_map/ppermute | solution.py:21
  (64 other events, 859.4 us)
Sparse Core Ops, SparseCore 0:
  92.9 43.3 all-gather.2
  150.7 65.0 reduce-scatter.6
  222.3 44.0 all-gather.4
  275.3 29.0 all-reduce.6
  308.5 66.2 reduce-scatter.8
where the time goes:
time: 479 us; the launch traced here: 478 us
  waiting for transfers between devices  238 us (50%)
  blocking collectives  130 us (27%)
  other arithmetic  40.6 us (8%)
  local copies, waits for them, and re-layouts  22.8 us (5%)
  matrix products  21 us (4%)
  between operations  15.2 us (3%)
  starting transfers between devices  11.2 us (2%)
    reduce_scatter x1, waiting for transfers between devices, body(): lax.psum_scatter(jnp.dot(weight_cut, grad_pre, preferred_element_type=jnp...  66.8 us
    unnamed x6, waiting for transfers between devices  62.8 us
    psum x1, blocking collectives, body(): lax.psum((jnp.sum(scaled_grad, axis=0), jnp.sum(scaled_grad * unit_norm,...  57.7 us
    all_gather x1, waiting for transfers between devices, body(): portion = lax.all_gather(scaled, 'chan', axis=0, tiled=True)  44 us
    all_gather x1, waiting for transfers between devices, body(): lax.all_gather(normed, 'chan', axis=0, tiled=True)  43.4 us
    psum x1, blocking collectives, body(): centre = lax.psum(jnp.sum(mixed_flat, axis=0), 'chan') / D  32.9 us
    psum x1, blocking collectives, body(): lax.psum(jnp.sum(jnp.square(mixed_flat - centre), axis=0), 'chan') / D  30 us
    psum x1, waiting for transfers between devices, body(): lax.psum(grad_w_in.astype(jnp.bfloat16), 'rows').astype(jnp.float32)  19.7 us
  transfers between devices with their start and end apart: 9, of which 6 were waited for; matrix products, arithmetic and copies ran while one was open for 4% of the time, Pallas kernels for 0%

commit v1 on v0

--- a/solution.py
+++ b/solution.py
@@ -8,6 +8,24 @@
 epsilon = 1e-06
 inv_root_two = 0.7071067811865476
 inv_root_two_pi = 0.3989422804014327
+
+
+def ring_gather(value, axis, dim):
+    ways, here, hop = (lax.axis_size(axis), lax.axis_index(axis), value.shape[dim])
+    shape = [n * ways if d == dim else n for d, n in enumerate(value.shape)]
+    full = lax.dynamic_update_slice_in_dim(
+        jnp.zeros(shape, value.dtype), value, here * hop, axis=dim
+    )
+    going_up = going_down = value
+    for far in range(1, ways // 2 + 1):
+        going_up = lax.ppermute(going_up, axis, [(d, (d + 1) % ways) for d in range(ways)])
+        full = lax.dynamic_update_slice_in_dim(full, going_up, (here - far) % ways * hop, axis=dim)
+        if 2 * far < ways:
+            going_down = lax.ppermute(going_down, axis, [(d, (d - 1) % ways) for d in range(ways)])
+            full = lax.dynamic_update_slice_in_dim(
+                full, going_down, (here + far) % ways * hop, axis=dim
+            )
+    return full
 
 
 def extended(block, sides, width):
@@ -83,7 +101,7 @@
     weight_cut = w_in
     pre_act = lax.dot_general(
         weight_cut,
-        lax.all_gather(normed, "chan", axis=0, tiled=True),
+        ring_gather(normed, "chan", 0),
         contract_lead,
         preferred_element_type=jnp.float32,
     )

time: 479 us -> 687 us (1.43)
  local copies, waits for them, and re-layouts: 22.8 us -> 133 us
  starting transfers between devices: 11.2 us -> 65.8 us
  waiting for transfers between devices: 238 us -> 271 us
    dynamic_update_slice x0 -> x16, local copies, waits for them, and re-layouts: none -> 104 us  [the longest x8 51.1 us: ring_gather(): lax.dynamic_update_slice_in_dim(full, going_up, (here - far) % ways * hop...]
    reduce_scatter x1 -> x0, waiting for transfers between devices: 66.8 us -> none  [body(): lax.psum_scatter(jnp.dot(weight_cut, grad_pre, preferred_element_type=jnp...]
    unnamed x6 -> x7, waiting for transfers between devices: 62.8 us -> 129 us
    ppermute x0 -> x15, starting transfers between devices: none -> 54.8 us  [the longest x8 42.4 us: ring_gather(): lax.ppermute(going_up, axis, [(d, (d + 1) % ways) for d in range(ways)])]
    ppermute x0 -> x15, waiting for transfers between devices: none -> 37.5 us  [the longest x8 37.5 us: ring_gather(): lax.ppermute(going_up, axis, [(d, (d + 1) % ways) for d in range(ways)])]
    unnamed x185 -> x215, local copies, waits for them, and re-layouts: 14.6 us -> 16.1 us
  transfers between devices with their start and end apart: 9 -> 24, of which waited for: 6 -> 13; matrix products, arithmetic and copies ran while one was open for 4% -> 19% of each run, Pallas kernels for 0% -> 0%
where the time goes in v1:
time: 687 us; the launch traced here: 680 us
  waiting for transfers between devices  271 us (39%)
  local copies, waits for them, and re-layouts  133 us (19%)
  blocking collectives  130 us (19%)
  starting transfers between devices  65.8 us (10%)
  other arithmetic  41.1 us (6%)
  matrix products  22.9 us (3%)
  between operations  15.5 us (2%)
    unnamed x7, waiting for transfers between devices  129 us
    psum x1, blocking collectives, body(): lax.psum((jnp.sum(scaled_grad, axis=0), jnp.sum(scaled_grad * unit_norm,...  58 us
    dynamic_update_slice x8, local copies, waits for them, and re-layouts, ring_gather(): lax.dynamic_update_slice_in_dim(full, going_up, (here - far) % ways * hop...  51.1 us
    dynamic_update_slice x7, local copies, waits for them, and re-layouts, ring_gather(): lax.dynamic_update_slice_in_dim(full, going_down, (here + far) % ways * h...  46.5 us
    all_gather x1, waiting for transfers between devices, body(): portion = lax.all_gather(scaled, 'chan', axis=0, tiled=True)  43.2 us
    ppermute x8, starting transfers between devices, ring_gather(): lax.ppermute(going_up, axis, [(d, (d + 1) % ways) for d in range(ways)])  42.4 us
    all_gather x1, waiting for transfers between devices, body(): lax.all_gather(normed, 'chan', axis=0, tiled=True)  40.5 us
    ppermute x8, waiting for transfers between devices, ring_gather(): lax.ppermute(going_up, axis, [(d, (d + 1) % ways) for d in range(ways)])  37.5 us
  transfers between devices with their start and end apart: 24, of which 13 were waited for; matrix products, arithmetic and copies ran while one was open for 19% of the time, Pallas kernels for 0%

profile of v1, /device:TPU:0, one launch (start us, length us, event | category | flops | bytes accessed | tf_op | source)
XLA Modules:
  0.0 679.6 jit_solution(9682842674159667044)
XLA Ops:
  20.2 8.3 %convert_reduce_fusion = (f32[16,128]{1,0:T(8,128)S(1)}, bf16[48,1,16,128]{3,2,1,0:T(8,128)(2,1)S(1)}) fusion(f32[48]{0:T(128)} %get-tuple-element.136, f32[48]{0:T(128)} %get-tuple-element.137, f32[48]{0:T(128)S(1)} %get-tuple-element.90, f32[48,1,22,128]{3,2,1,0:T(8,128)S(1)} %maximum_convert_fusion, f32[48]{0:T(128)S(1)} %get-tuple-element.91, ...), kind=kLoop, calls=%fused_computation.339 | loop fusion | flops 9828352 | bytes 3571264 | tf_op jit(solution)/shard_map/reduce_sum | solution.py:96
  28.9 32.8 %psum.63 = f32[2048]{0:T(1024)S(1)} all-reduce(f32[2048]{0:T(1024)S(1)} %bitcast.312), channel_id=1, replica_groups=mesh['chan'=16,'rows'=2] {'chan'}, use_global_device_ids=true, to_apply=%region_1.2 | all-reduce | flops 2048 | bytes 16384 | tf_op jit(solution)/shard_map/psum | solution.py:96
  62.1 30.0 %psum.64 = f32[2048]{0:T(1024)S(1)} all-reduce(f32[2048]{0:T(1024)S(1)} %bitcast.313), channel_id=1, replica_groups=mesh['chan'=16,'rows'=2] {'chan'}, use_global_device_ids=true, to_apply=%region_3.4 | all-reduce | flops 2048 | bytes 16384 | tf_op jit(solution)/shard_map/psum | solution.py:97
  97.3 7.0 %collective-permute-done.2 = bf16[48,2048]{0,1:T(8,128)(2,1)S(1)} collective-permute-done((bf16[48,2048]{0,1:T(8,128)(2,1)S(1)}, bf16[48,2048]{0,1:T(8,128)(2,1)S(1)}, u32[]{:S(2)}, u32[]{:S(2)}) %collective-permute-start.2) | collective-permute-done | bytes 196640 | tf_op jit(solution)/shard_map/ppermute | solution.py:21
  108.7 7.0 %collective-permute-done.4 = bf16[48,2048]{0,1:T(8,128)(2,1)S(1)} collective-permute-done((bf16[48,2048]{0,1:T(8,128)(2,1)S(1)}, bf16[48,2048]{0,1:T(8,128)(2,1)S(1)}, u32[]{:S(2)}, u32[]{:S(2)}) %collective-permute-start.4) | collective-permute-done | bytes 196640 | tf_op jit(solution)/shard_map/ppermute | solution.py:21
  120.1 6.8 %collective-permute-done.6 = bf16[48,2048]{0,1:T(8,128)(2,1)S(1)} collective-permute-done((bf16[48,2048]{0,1:T(8,128)(2,1)S(1)}, bf16[48,2048]{0,1:T(8,128)(2,1)S(1)}, u32[]{:S(2)}, u32[]{:S(2)}) %collective-permute-start.6) | collective-permute-done | bytes 196640 | tf_op jit(solution)/shard_map/ppermute | solution.py:21
  131.5 6.9 %collective-permute-done.8 = bf16[48,2048]{0,1:T(8,128)(2,1)S(1)} collective-permute-done((bf16[48,2048]{0,1:T(8,128)(2,1)S(1)}, bf16[48,2048]{0,1:T(8,128)(2,1)S(1)}, u32[]{:S(2)}, u32[]{:S(2)}) %collective-permute-start.8) | collective-permute-done | bytes 196640 | tf_op jit(solution)/shard_map/ppermute | solution.py:21
  138.4 7.1 %collective-permute-start.10 = (bf16[48,2048]{0,1:T(8,128)(2,1)S(1)}, bf16[48,2048]{0,1:T(8,128)(2,1)S(1)}, u32[]{:S(2)}, u32[]{:S(2)}) collective-permute-start(bf16[48,2048]{0,1:T(8,128)(2,1)S(1)} %collective-permute-done.8), channel_id=1, source_target_pairs={{0,2},{2,4},{4,6},{6,8},{8,10},{10,12},{12,14},{14,16},{16,18},{18... | collective-permute-start | bytes 589832 | tf_op jit(solution)/shard_map/ppermute | solution.py:21
  149.8 9.9 %collective-permute-start.12 = (bf16[48,2048]{0,1:T(8,128)(2,1)S(1)}, bf16[48,2048]{0,1:T(8,128)(2,1)S(1)}, u32[]{:S(2)}, u32[]{:S(2)}) collective-permute-start(bf16[48,2048]{0,1:T(8,128)(2,1)S(1)} %collective-permute-done.10), channel_id=1, source_target_pairs={{0,2},{2,4},{4,6},{6,8},{8,10},{10,12},{12,14},{14,16},{16,18},{18... | collective-permute-start | bytes 589832 | tf_op jit(solution)/shard_map/ppermute | solution.py:21
  162.5 11.4 %collective-permute-start.14 = (bf16[48,2048]{0,1:T(8,128)(2,1)S(1)}, bf16[48,2048]{0,1:T(8,128)(2,1)}, u32[]{:S(2)}, u32[]{:S(2)}) collective-permute-start(bf16[48,2048]{0,1:T(8,128)(2,1)S(1)} %collective-permute-done.12), channel_id=1, source_target_pairs={{0,2},{2,4},{4,6},{6,8},{8,10},{10,12},{12,14},{14,16},{16,18},{18... | collective-permute-start | bytes 589832 | tf_op jit(solution)/shard_map/ppermute | solution.py:21
  176.8 8.3 %collective-permute-start.16 = (bf16[48,2048]{0,1:T(8,128)(2,1)}, bf16[48,2048]{0,1:T(8,128)(2,1)}, u32[]{:S(2)}, u32[]{:S(2)}) collective-permute-start(bf16[48,2048]{0,1:T(8,128)(2,1)} %collective-permute-done.14), channel_id=1, source_target_pairs={{0,2},{2,4},{4,6},{6,8},{8,10},{10,12},{12,14},{14,16},{16,18},{18... | collective-permute-start | bytes 589832 | tf_op jit(solution)/shard_map/ppermute | solution.py:21
  199.0 6.6 dynamic_update_slice.50
  211.7 6.5 dynamic_update_slice.52
  218.2 6.5 dynamic_update_slice.53
  224.8 6.8 %dynamic_update_slice.54 = bf16[768,2048]{0,1:T(8,128)(2,1)} dynamic-update-slice(bf16[768,2048]{0,1:T(8,128)(2,1)} %dynamic_update_slice.53, bf16[48,2048]{0,1:T(8,128)(2,1)} %copy-done.10, s32[]{:T(128)S(6)} %select_n.123, s32[]{:T(128)} %constant.137.clone.1) | dynamic-update-slice | bytes 393220 | tf_op jit(solution)/shard_map/dynamic_update_slice | solution.py:25
  231.6 6.5 dynamic_update_slice.55
  238.1 6.5 dynamic_update_slice.56
  244.6 6.8 %dynamic_update_slice.57 = bf16[768,2048]{0,1:T(8,128)(2,1)} dynamic-update-slice(bf16[768,2048]{0,1:T(8,128)(2,1)} %dynamic_update_slice.56, bf16[48,2048]{0,1:T(8,128)(2,1)} %copy-done.15, s32[]{:T(128)S(6)} %select_n.129, s32[]{:T(128)} %constant.137.clone.1) | dynamic-update-slice | bytes 393220 | tf_op jit(solution)/shard_map/dynamic_update_slice | solution.py:22
  251.4 6.5 dynamic_update_slice.58
  257.9 6.5 dynamic_update_slice.59
  264.4 6.8 dynamic_update_slice.60
  271.2 6.8 %dynamic_update_slice.61 = bf16[768,2048]{0,1:T(8,128)(2,1)} dynamic-update-slice(bf16[768,2048]{0,1:T(8,128)(2,1)} %dynamic_update_slice.60, bf16[48,2048]{0,1:T(8,128)(2,1)} %collective-permute-done.14, s32[]{:T(128)S(6)} %select_n.137, s32[]{:T(128)} %constant.137.clone.1) | dynamic-update-slice | bytes 393220 | tf_op jit(solution)/shard_map/dynamic_update_slice | solution.py:22
  278.0 6.8 %dynamic_update_slice.62 = bf16[768,2048]{0,1:T(8,128)(2,1)} dynamic-update-slice(bf16[768,2048]{0,1:T(8,128)(2,1)} %dynamic_update_slice.61, bf16[48,2048]{0,1:T(8,128)(2,1)} %collective-permute-done.15, s32[]{:T(128)S(6)} %select_n.139, s32[]{:T(128)} %constant.137.clone.1) | dynamic-update-slice | bytes 393220 | tf_op jit(solution)/shard_map/dynamic_update_slice | solution.py:25
  290.8 7.0 %fusion.6 = (bf16[192,2048]{1,0:T(8,128)(2,1)S(1)}, f32[192,2048]{1,0:T(8,128)}) fusion(bf16[768,2048]{0,1:T(8,128)(2,1)} %dynamic_update_slice.63, bf16[768,192]{0,1:T(8,128)(2,1)S(1)} %copy-done), kind=kOutput, calls=%fused_computation.145 | convolution fusion | flops 629538816 | bytes 5799936 | tf_op jit(solution)/shard_map/dot_general | solution.py:102
  309.9 62.3 %reduce-scatter.7.cloned.1.call-done = bf16[48,2048]{1,0:T(8,128)(2,1)} async-done(((bf16[768,2048]{1,0:T(8,128)(2,1)}), bf16[48,2048]{1,0:T(8,128)(2,1)}) %reduce-scatter.7.cloned.1.call-update) | async-done | bytes 196624
  380.1 43.2 %all-gather.3.cloned.1.call-done = bf16[768,2048]{1,0:T(8,128)(2,1)} async-done(((bf16[48,2048]{1,0:T(8,128)(2,1)}), bf16[768,2048]{1,0:T(8,128)(2,1)}) %all-gather.3.cloned.1.call-update) | async-done | bytes 3145744 | tf_op jit(solution)/shard_map/all_gather | solution.py:124
  429.9 40.5 %all-gather.5.cloned.1.call-done = bf16[768,2048]{1,0:T(8,128)(2,1)} async-done(((bf16[48,2048]{1,0:T(8,128)(2,1)}), bf16[768,2048]{1,0:T(8,128)(2,1)}) %all-gather.5.cloned.1.call-update) | async-done | bytes 3145744 | tf_op jit(solution)/shard_map/all_gather | solution.py:134
  483.8 19.7 %all-reduce.7.cloned.1.call-done = (bf16[768,192]{0,1:T(8,128)(2,1)}, bf16[192,768]{1,0:T(8,128)(2,1)}) async-done(((bf16[768,192]{0,1:T(8,128)(2,1)}, bf16[192,768]{1,0:T(8,128)(2,1)}), (bf16[768,192]{0,1:T(8,128)(2,1)}, bf16[192,768]{1,0:T(8,128)(2,1)})) %all-reduce.7.cloned.1.call-update) | async-done | bytes 589840 | tf_op jit(solution)/shard_map/psum | solution.py:161
  507.1 66.8 %reduce-scatter.9.cloned.1.call-done = bf16[48,2048]{1,0:T(8,128)(2,1)} async-done(((bf16[768,2048]{1,0:T(8,128)(2,1)}), bf16[48,2048]{1,0:T(8,128)(2,1)}) %reduce-scatter.9.cloned.1.call-update) | async-done | bytes 196624
  576.5 58.0 %all-reduce.2 = (f32[2048]{0:T(1024)S(1)}, f32[2048]{0:T(1024)S(1)}) all-reduce(f32[2048]{0:T(1024)S(1)} %get-tuple-element.22, f32[2048]{0:T(1024)S(1)} %get-tuple-element.72), channel_id=1, replica_groups=mesh['chan'=16,'rows'=2] {'chan'}, use_global_device_ids=true, to_apply=%region_9.10 | all-reduce | flops 4096 | bytes 32768 | tf_op jit(solution)/shard_map/psum | solution.py:148
  652.3 9.2 %all-reduce.3 = (bf16[48,7,7]{0,2,1:T(8,128)(2,1)S(1)}, bf16[48]{0:T(256)(128)(2,1)S(1)}, bf16[48]{0:T(256)(128)(2,1)S(1)}) all-reduce(bf16[48,7,7]{0,2,1:T(8,128)(2,1)S(1)} %constant_dynamic-update-slice_fusion, bf16[48]{0:T(256)(128)(2,1)S(1)} %get-tuple-element.21, ...), channel_id=1, replica_groups=mesh['chan'=16,'rows'=2] {'rows'}, use_global_device_ids=true, to_apply=%region_59.60 | all-reduce | flops 2448 | bytes 9792 | tf_op jit(solution)/shard_map/psum | solution.py:163
  663.8 9.1 %fusion.167 = bf16[48,1,16,128]{3,2,1,0:T(8,128)(2,1)} fusion(f32[48,1,22,128]{3,2,1,0:T(8,128)S(1)} %maximum_convert_fusion.1, f32[48]{0:T(128)} %get-tuple-element.136, f32[48]{0:T(128)} %get-tuple-element.137, f32[48]{0:T(128)S(1)} %get-tuple-element.90, f32[48]{0:T(128)S(1)} %get-tuple-element.91, f32[48]{0:T(128)S(1)} %get-tuple-element.92, ...), kind=kLoop, calls=%fused_computation.323 | loop fusion | flops 9830400 | bytes 3759680 | tf_op jit(solution)/shard_map/convert_element_type | solution.py:158
  (302 shorter events, 133.1 us)
Async XLA Ops:
  7.2 283.6 %copy-start = (bf16[768,192]{0,1:T(8,128)(2,1)S(1)}, bf16[768,192]{0,1:T(8,128)(2,1)}, u32[]{:S(2)}) copy-start(bf16[768,192]{0,1:T(8,128)(2,1)} %param.10) | copy-start | bytes 884740
  7.2 365.1 %reduce-scatter.7.cloned.1.call-start = ((), (), s32[]{:S(2)}) async-start(), calls=%async_computation.4 | async-start | bytes 3342336
  8.3 10.0 %collective-permute-start = (bf16[48,1,3,128]{3,2,1,0:T(4,128)(2,1)S(1)}, bf16[48,1,3,128]{3,2,1,0:T(4,128)(2,1)S(1)}, u32[]{:S(2)}, u32[]{:S(2)}) collective-permute-start(bf16[48,1,3,128]{3,2,1,0:T(4,128)(2,1)S(1)} %get-tuple-element.87), channel_id=1, source_target_pairs={{0,1},{2,3},{4,5},{6,7},{8,9},{10,11},{12,13},{14,15},{16,17},{18,... | collective-permute-start | bytes 110600 | tf_op jit(solution)/shard_map/ppermute | solution.py:36
  13.1 6.0 collective-permute-start.1
  20.2 72.0 %copy-start.22 = (f32[48]{0:T(128)S(1)}, f32[48]{0:T(128)}, u32[]{:S(2)}) copy-start(f32[48]{0:T(128)} %param.9) | copy-start | bytes 580
  92.8 11.5 %collective-permute-start.2 = (bf16[48,2048]{0,1:T(8,128)(2,1)S(1)}, bf16[48,2048]{0,1:T(8,128)(2,1)S(1)}, u32[]{:S(2)}, u32[]{:S(2)}) collective-permute-start(bf16[48,2048]{0,1:T(8,128)(2,1)S(1)} %multiply_convert_fusion), channel_id=1, source_target_pairs={{0,2},{2,4},{4,6},{6,8},{8,10},{10,12},{12,14},{14,16},{16,18},{18... | collective-permute-start | bytes 589832 | tf_op jit(solution)/shard_map/ppermute | solution.py:21
  92.8 11.4 %collective-permute-start.3 = (bf16[48,2048]{0,1:T(8,128)(2,1)S(1)}, bf16[48,2048]{0,1:T(8,128)(2,1)S(1)}, u32[]{:S(2)}, u32[]{:S(2)}) collective-permute-start(bf16[48,2048]{0,1:T(8,128)(2,1)S(1)} %multiply_convert_fusion), channel_id=1, source_target_pairs={{0,30},{2,0},{4,2},{6,4},{8,6},{10,8},{12,10},{14,12},{16,14},{18,... | collective-permute-start | bytes 589832 | tf_op jit(solution)/shard_map/ppermute | solution.py:24
  104.2 11.4 %collective-permute-start.4 = (bf16[48,2048]{0,1:T(8,128)(2,1)S(1)}, bf16[48,2048]{0,1:T(8,128)(2,1)S(1)}, u32[]{:S(2)}, u32[]{:S(2)}) collective-permute-start(bf16[48,2048]{0,1:T(8,128)(2,1)S(1)} %collective-permute-done.2), channel_id=1, source_target_pairs={{0,2},{2,4},{4,6},{6,8},{8,10},{10,12},{12,14},{14,16},{16,18},{18... | collective-permute-start | bytes 589832 | tf_op jit(solution)/shard_map/ppermute | solution.py:21
  104.2 12.8 %collective-permute-start.5 = (bf16[48,2048]{0,1:T(8,128)(2,1)S(1)}, bf16[48,2048]{0,1:T(8,128)(2,1)S(1)}, u32[]{:S(2)}, u32[]{:S(2)}) collective-permute-start(bf16[48,2048]{0,1:T(8,128)(2,1)S(1)} %collective-permute-done.3), channel_id=1, source_target_pairs={{0,30},{2,0},{4,2},{6,4},{8,6},{10,8},{12,10},{14,12},{16,14},{18,... | collective-permute-start | bytes 589832 | tf_op jit(solution)/shard_map/ppermute | solution.py:24
  115.6 11.3 %collective-permute-start.6 = (bf16[48,2048]{0,1:T(8,128)(2,1)S(1)}, bf16[48,2048]{0,1:T(8,128)(2,1)S(1)}, u32[]{:S(2)}, u32[]{:S(2)}) collective-permute-start(bf16[48,2048]{0,1:T(8,128)(2,1)S(1)} %collective-permute-done.4), channel_id=1, source_target_pairs={{0,2},{2,4},{4,6},{6,8},{8,10},{10,12},{12,14},{14,16},{16,18},{18... | collective-permute-start | bytes 589832 | tf_op jit(solution)/shard_map/ppermute | solution.py:21
  117.0 14.2 %collective-permute-start.7 = (bf16[48,2048]{0,1:T(8,128)(2,1)S(1)}, bf16[48,2048]{0,1:T(8,128)(2,1)S(1)}, u32[]{:S(2)}, u32[]{:S(2)}) collective-permute-start(bf16[48,2048]{0,1:T(8,128)(2,1)S(1)} %collective-permute-done.5), channel_id=1, source_target_pairs={{0,30},{2,0},{4,2},{6,4},{8,6},{10,8},{12,10},{14,12},{16,14},{18,... | collective-permute-start | bytes 589832 | tf_op jit(solution)/shard_map/ppermute | solution.py:24
  127.0 11.4 %collective-permute-start.8 = (bf16[48,2048]{0,1:T(8,128)(2,1)S(1)}, bf16[48,2048]{0,1:T(8,128)(2,1)S(1)}, u32[]{:S(2)}, u32[]{:S(2)}) collective-permute-start(bf16[48,2048]{0,1:T(8,128)(2,1)S(1)} %collective-permute-done.6), channel_id=1, source_target_pairs={{0,2},{2,4},{4,6},{6,8},{8,10},{10,12},{12,14},{14,16},{16,18},{18... | collective-permute-start | bytes 589832 | tf_op jit(solution)/shard_map/ppermute | solution.py:21
  131.2 14.2 %collective-permute-start.9 = (bf16[48,2048]{0,1:T(8,128)(2,1)S(1)}, bf16[48,2048]{0,1:T(8,128)(2,1)S(1)}, u32[]{:S(2)}, u32[]{:S(2)}) collective-permute-start(bf16[48,2048]{0,1:T(8,128)(2,1)S(1)} %collective-permute-done.7), channel_id=1, source_target_pairs={{0,30},{2,0},{4,2},{6,4},{8,6},{10,8},{12,10},{14,12},{16,14},{18,... | collective-permute-start | bytes 589832 | tf_op jit(solution)/shard_map/ppermute | solution.py:24
  138.4 11.4 %collective-permute-start.10 = (bf16[48,2048]{0,1:T(8,128)(2,1)S(1)}, bf16[48,2048]{0,1:T(8,128)(2,1)S(1)}, u32[]{:S(2)}, u32[]{:S(2)}) collective-permute-start(bf16[48,2048]{0,1:T(8,128)(2,1)S(1)} %collective-permute-done.8), channel_id=1, source_target_pairs={{0,2},{2,4},{4,6},{6,8},{8,10},{10,12},{12,14},{14,16},{16,18},{18... | collective-permute-start | bytes 589832 | tf_op jit(solution)/shard_map/ppermute | solution.py:21
  145.5 14.2 %collective-permute-start.11 = (bf16[48,2048]{0,1:T(8,128)(2,1)S(1)}, bf16[48,2048]{0,1:T(8,128)(2,1)S(1)}, u32[]{:S(2)}, u32[]{:S(2)}) collective-permute-start(bf16[48,2048]{0,1:T(8,128)(2,1)S(1)} %collective-permute-done.9), channel_id=1, source_target_pairs={{0,30},{2,0},{4,2},{6,4},{8,6},{10,8},{12,10},{14,12},{16,14},{18,... | collective-permute-start | bytes 589832 | tf_op jit(solution)/shard_map/ppermute | solution.py:24
  149.8 12.7 %collective-permute-start.12 = (bf16[48,2048]{0,1:T(8,128)(2,1)S(1)}, bf16[48,2048]{0,1:T(8,128)(2,1)S(1)}, u32[]{:S(2)}, u32[]{:S(2)}) collective-permute-start(bf16[48,2048]{0,1:T(8,128)(2,1)S(1)} %collective-permute-done.10), channel_id=1, source_target_pairs={{0,2},{2,4},{4,6},{6,8},{8,10},{10,12},{12,14},{14,16},{16,18},{18... | collective-permute-start | bytes 589832 | tf_op jit(solution)/shard_map/ppermute | solution.py:21
  159.7 14.2 %collective-permute-start.13 = (bf16[48,2048]{0,1:T(8,128)(2,1)S(1)}, bf16[48,2048]{0,1:T(8,128)(2,1)}, u32[]{:S(2)}, u32[]{:S(2)}) collective-permute-start(bf16[48,2048]{0,1:T(8,128)(2,1)S(1)} %collective-permute-done.11), channel_id=1, source_target_pairs={{0,30},{2,0},{4,2},{6,4},{8,6},{10,8},{12,10},{14,12},{16,14},{18,... | collective-permute-start | bytes 589832 | tf_op jit(solution)/shard_map/ppermute | solution.py:24
  162.5 14.3 %collective-permute-start.14 = (bf16[48,2048]{0,1:T(8,128)(2,1)S(1)}, bf16[48,2048]{0,1:T(8,128)(2,1)}, u32[]{:S(2)}, u32[]{:S(2)}) collective-permute-start(bf16[48,2048]{0,1:T(8,128)(2,1)S(1)} %collective-permute-done.12), channel_id=1, source_target_pairs={{0,2},{2,4},{4,6},{6,8},{8,10},{10,12},{12,14},{14,16},{16,18},{18... | collective-permute-start | bytes 589832 | tf_op jit(solution)/shard_map/ppermute | solution.py:21
  173.9 104.0 %collective-permute-start.15 = (bf16[48,2048]{0,1:T(8,128)(2,1)}, bf16[48,2048]{0,1:T(8,128)(2,1)}, u32[]{:S(2)}, u32[]{:S(2)}) collective-permute-start(bf16[48,2048]{0,1:T(8,128)(2,1)} %collective-permute-done.13), channel_id=1, source_target_pairs={{0,30},{2,0},{4,2},{6,4},{8,6},{10,8},{12,10},{14,12},{16,14},{18,... | collective-permute-start | bytes 589832 | tf_op jit(solution)/shard_map/ppermute | solution.py:24
  176.8 108.0 %collective-permute-start.16 = (bf16[48,2048]{0,1:T(8,128)(2,1)}, bf16[48,2048]{0,1:T(8,128)(2,1)}, u32[]{:S(2)}, u32[]{:S(2)}) collective-permute-start(bf16[48,2048]{0,1:T(8,128)(2,1)} %collective-permute-done.14), channel_id=1, source_target_pairs={{0,2},{2,4},{4,6},{6,8},{8,10},{10,12},{12,14},{14,16},{16,18},{18... | collective-permute-start | bytes 589832 | tf_op jit(solution)/shard_map/ppermute | solution.py:21
  305.5 68.7 %copy-start.101 = (f32[48]{0:T(128)S(1)}, f32[48]{0:T(128)}, u32[]{:S(2)}) copy-start(f32[48]{0:T(128)} %param.12) | copy-start | bytes 580
  305.5 117.8 %all-gather.3.cloned.1.call-start = ((), (), s32[]{:S(2)}) async-start(), calls=%async_computation.2 | async-start | bytes 3342336 | tf_op jit(solution)/shard_map/all_gather | solution.py:124
  379.1 91.4 %all-gather.5.cloned.1.call-start = ((), (), s32[]{:S(2)}) async-start(), calls=%async_computation.3 | async-start | bytes 3342336 | tf_op jit(solution)/shard_map/all_gather | solution.py:134
  380.0 47.3 %copy-start.21 = (bf16[192,768]{1,0:T(8,128)(2,1)S(1)}, bf16[192,768]{1,0:T(8,128)(2,1)}, u32[]{:S(2)}) copy-start(bf16[192,768]{1,0:T(8,128)(2,1)} %param.11) | copy-start | bytes 884740
  380.0 123.4 %all-reduce.7.cloned.1.call-start = ((), (), s32[]{:S(2)}) async-start(), calls=%async_computation.6 | async-start | bytes 1179648 | tf_op jit(solution)/shard_map/psum | solution.py:161
  474.3 99.6 %reduce-scatter.9.cloned.1.call-start = ((), (), s32[]{:S(2)}) async-start(), calls=%async_computation.5 | async-start | bytes 3342336
  644.2 19.2 %copy-start.4 = (bf16[48,1,16,128]{3,2,1,0:T(8,128)(2,1)S(1)}, bf16[48,1,16,128]{3,2,1,0:T(8,128)(2,1)}, u32[]{:S(2)}) copy-start(bf16[48,1,16,128]{3,2,1,0:T(8,128)(2,1)} %param.13) | copy-start | bytes 589828
  644.2 19.2 %copy-start.24 = (f32[48]{0:T(128)S(1)}, f32[48]{0:T(128)}, u32[]{:S(2)}) copy-start(f32[48]{0:T(128)} %copy-done.23) | copy-start | bytes 580
  644.2 19.2 %copy-start.26 = (f32[48]{0:T(128)S(1)}, f32[48]{0:T(128)}, u32[]{:S(2)}) copy-start(f32[48]{0:T(128)} %copy-done.25) | copy-start | bytes 580
  644.2 19.2 %copy-start.28 = (f32[48]{0:T(128)S(1)}, f32[48]{0:T(128)}, u32[]{:S(2)}) copy-start(f32[48]{0:T(128)} %copy-done.27) | copy-start | bytes 580
  647.4 15.8 %collective-permute-start.17 = (bf16[48,1,3,128]{3,2,1,0:T(4,128)(2,1)S(1)}, bf16[48,1,3,128]{3,2,1,0:T(4,128)(2,1)S(1)}, u32[]{:S(2)}, u32[]{:S(2)}) collective-permute-start(bf16[48,1,3,128]{3,2,1,0:T(4,128)(2,1)S(1)} %get-tuple-element.85), channel_id=1, source_target_pairs={{0,1},{2,3},{4,5},{6,7},{8,9},{10,11},{12,13},{14,15},{16,17},{18,... | collective-permute-start | bytes 110600 | tf_op jit(solution)/shard_map/ppermute | solution.py:36
  650.8 12.4 %collective-permute-start.18 = (bf16[48,1,3,128]{3,2,1,0:T(4,128)(2,1)S(1)}, bf16[48,1,3,128]{3,2,1,0:T(4,128)(2,1)S(1)}, u32[]{:S(2)}, u32[]{:S(2)}) collective-permute-start(bf16[48,1,3,128]{3,2,1,0:T(4,128)(2,1)S(1)} %get-tuple-element.86), channel_id=1, source_target_pairs={{1,0},{3,2},{5,4},{7,6},{9,8},{11,10},{13,12},{15,14},{17,16},{19,... | collective-permute-start | bytes 110600 | tf_op jit(solution)/shard_map/ppermute | solution.py:39
  (94 other events, 1313.7 us)
Sparse Core Ops, SparseCore 0:
  305.6 66.5 reduce-scatter.6
  379.2 44.0 all-gather.2
  426.2 44.2 all-gather.4
  474.4 29.0 all-reduce.6
  507.6 66.2 reduce-scatter.8
